TPU v7x, 32 devices: a whole 2x2x4 slice. The times are simulated.
32 devices in a mesh: rep: 1, seq: 8 (over z, y), head: 2 (over x), sub: 2 (over core).
Axes of the slice: x: 2, y: 2, z: 4, core: 2. Of those that a mesh axis runs over, the one named last changes fastest.
Arguments:
- head_query_rows: bfloat16 [2048, 2048], P(('rep', 'seq', 'sub'), 'head'), may hold values from -6 to 6, as said below
- head_key_rows: bfloat16 [2048, 2048], P(('rep', 'seq', 'sub'), 'head'), may hold values from -6 to 6, as said below
- head_value_rows: bfloat16 [2048, 2048], P(('rep', 'seq', 'sub'), 'head'), may hold values from -6 to 6
- output_gradient: bfloat16 [2048, 4096], P(('rep', 'seq', 'sub'), 'head'), may hold values from -6 to 6
- output_matrix: bfloat16 [2048, 4096], P('head', 'sub'), may hold values from -0.125 to 0.125
- adapter_down_weight: bfloat16 [2048, 16], P('head'), may hold values from -0.125 to 0.125
- adapter_up_weight: bfloat16 [16, 4096], replicated, may hold values from -0.09375 to 0.09375
Outputs:
- query_gradient: bfloat16 [2048, 2048], P(('rep', 'seq', 'sub'), 'head')
- key_gradient: bfloat16 [2048, 2048], P(('rep', 'seq', 'sub'), 'head')
- value_gradient: bfloat16 [2048, 2048], P(('rep', 'seq', 'sub'), 'head')
- adapter_down_gradient: float32 [2048, 16], P(('rep', 'head'))
- adapter_up_gradient: float32 [16, 4096], P('rep', 'head')
Inputs may be any that keep to these rules, and one draw needn't show every extreme that they name: `head_query_rows`: entries of the queries are real values within the range. `head_key_rows`: entries of the keys are real values within the range.
All inputs are finite; a program needn't handle non-finite values.
Results may differ from a plain program's by a relative error of at most 0.029.
Values may be sent and summed in bfloat16 or wider, within the bound.
A program may use at most 64 MiB of HBM per device.

v0:
```python
import jax
import jax.numpy as jnp
from jax import lax
from jax.sharding import PartitionSpec as P

HD = 128
GROUP = 2048


def passed_along(value, axis, by):
    peers = lax.axis_size(axis)
    return lax.ppermute(value, axis, [(i, (i + by) % peers) for i in range(peers)])


def placed_visible(row_count, window_rows, seq_total, first_row, back_rows, roll_by):
    query_pos = first_row + lax.broadcasted_iota(jnp.int32, (row_count, window_rows), 0)
    key_pos = (
        first_row
        - back_rows
        + seq_total
        + lax.broadcasted_iota(jnp.int32, (row_count, window_rows), 1)
    ) % seq_total
    query_order = (query_pos - roll_by + seq_total) % seq_total
    key_order = (key_pos - roll_by + seq_total) % seq_total
    return (query_order // GROUP == key_order // GROUP) & (key_order <= query_order)


def softmax_rows(query_head, keys_head, visible):
    scores = lax.dot_general(
        query_head, keys_head, (((1,), (1,)), ((), ())), preferred_element_type=jnp.float32
    )
    scores = jnp.where(visible, scores * HD ** (-0.5), -jnp.inf)
    highest = jnp.max(scores, axis=1, keepdims=True)
    powers = jnp.exp(scores - highest)
    return powers / jnp.sum(powers, axis=1, keepdims=True)


def head_forward(query_head, window_head, visible):
    prob = softmax_rows(query_head, window_head[0], visible)
    return jnp.dot(
        prob.astype(jnp.bfloat16), window_head[1], preferred_element_type=jnp.float32
    ).astype(jnp.bfloat16)


def head_backward(query_head, window_head, dout_head, visible):
    prob = softmax_rows(query_head, window_head[0], visible)
    prob_lo = prob.astype(jnp.bfloat16)
    dprob = lax.dot_general(
        dout_head, window_head[1], (((1,), (1,)), ((), ())), preferred_element_type=jnp.float32
    )
    delta = jnp.sum(prob * dprob, axis=1, keepdims=True)
    dscore = (prob * (dprob - delta) * HD ** (-0.5)).astype(jnp.bfloat16)
    grad_q = jnp.dot(dscore, window_head[0], preferred_element_type=jnp.float32).astype(
        jnp.bfloat16
    )
    grad_k = lax.dot_general(
        dscore, query_head, (((0,), (0,)), ((), ())), preferred_element_type=jnp.float32
    )
    grad_v = lax.dot_general(
        prob_lo, dout_head, (((0,), (0,)), ((), ())), preferred_element_type=jnp.float32
    )
    return (grad_q, jnp.stack((grad_k.astype(jnp.bfloat16), grad_v.astype(jnp.bfloat16))))


def attend_window(query_rows, window, dout_rows, visible):
    row_count, feat_count = query_rows.shape
    heads_here = feat_count // HD
    window_rows = window.shape[1]
    window_heads = window.reshape(2, window_rows, heads_here, HD).transpose(2, 0, 1, 3)
    query_heads = query_rows.reshape(row_count, heads_here, HD).transpose(1, 0, 2)
    dout_heads = dout_rows.reshape(row_count, heads_here, HD).transpose(1, 0, 2)
    attn_heads = lax.map(
        lambda pieces: head_forward(pieces[0], pieces[1], visible), (query_heads, window_heads)
    )
    grad_q_heads, pair_heads = lax.map(
        lambda pieces: head_backward(pieces[0], pieces[1], pieces[2], visible),
        (query_heads, window_heads, dout_heads),
    )
    attention_output = attn_heads.transpose(1, 0, 2).reshape(row_count, feat_count)
    query_gradient = grad_q_heads.transpose(1, 0, 2).reshape(row_count, feat_count)
    pair_grads = pair_heads.transpose(1, 2, 0, 3).reshape(2, window_rows, feat_count)
    return (attention_output, query_gradient, pair_grads)


def on_device(
    head_query_rows,
    head_key_rows,
    head_value_rows,
    output_gradient,
    output_matrix,
    adapter_down_weight,
    adapter_up_weight,
):
    tokens_dev, feat_dev = head_query_rows.shape
    head_index = lax.axis_index("head")
    shifted = head_index >= lax.axis_size("head") // 2
    total_gradient = lax.all_gather(output_gradient, "head", axis=1, tiled=True)
    projected_output = lax.dot_general(
        total_gradient,
        lax.all_gather(output_matrix, "sub", axis=1, tiled=True),
        (((1,), (1,)), ((), ())),
        preferred_element_type=jnp.float32,
    )
    adapter_upward = lax.dot_general(
        total_gradient,
        adapter_up_weight,
        (((1,), (1,)), ((), ())),
        preferred_element_type=jnp.float32,
    )
    adapter_backward = jnp.dot(
        adapter_upward, adapter_down_weight.astype(jnp.float32).T, precision=lax.Precision.HIGHEST
    )
    attention_gradient = (projected_output + 2.0 * adapter_backward).astype(jnp.bfloat16)
    sub_count = lax.axis_size("sub")
    block_rows = tokens_dev * sub_count
    seq_total = block_rows * lax.axis_size("seq")
    reach = max(GROUP // block_rows - 1, 1)
    roll_by = jnp.where(shifted, GROUP // 2, 0)
    stacked = jnp.stack((head_query_rows, head_key_rows, head_value_rows, attention_gradient))
    moved = lax.all_to_all(stacked, "sub", split_axis=2, concat_axis=1, tiled=True)
    own_pair = moved[1:3]
    received = [passed_along(own_pair, "seq", distance) for distance in range(reach, 0, -1)]
    window = jnp.concatenate(received + [own_pair], axis=1)
    first_row = lax.axis_index("seq") * block_rows
    visible = placed_visible(
        block_rows, window.shape[1], seq_total, first_row, reach * block_rows, roll_by
    )
    attn_local, grad_q_local, pair_grads = attend_window(moved[0], window, moved[3], visible)
    running = pair_grads[:, reach * block_rows :].astype(jnp.float32)
    for distance in range(1, reach + 1):
        begin_row = (reach - distance) * block_rows
        block_terms = pair_grads[:, begin_row : begin_row + block_rows]
        returned = passed_along(block_terms, "seq", -distance)
        running = running + returned.astype(jnp.float32)
    pair_local = running.astype(jnp.bfloat16)
    back = jnp.stack((attn_local, grad_q_local, pair_local[0], pair_local[1]))
    restored = lax.all_to_all(back, "sub", split_axis=1, concat_axis=2, tiled=True)
    attention_output = restored[0]
    query_gradient = restored[1]
    key_gradient = restored[2]
    value_gradient = restored[3]
    middle_piece = jnp.dot(
        attention_output, adapter_down_weight, preferred_element_type=jnp.float32
    )
    down_gradient_part = 2.0 * jnp.dot(
        attention_output.astype(jnp.float32).T, adapter_upward, precision=lax.Precision.HIGHEST
    )
    adapter_middle = lax.psum(middle_piece, "head")
    up_gradient_part = 2.0 * jnp.dot(
        adapter_middle.T, output_gradient.astype(jnp.float32), precision=lax.Precision.HIGHEST
    )
    adapter_down_gradient, adapter_up_gradient = lax.psum(
        (down_gradient_part, up_gradient_part), ("seq", "sub")
    )
    return (
        query_gradient,
        key_gradient,
        value_gradient,
        adapter_down_gradient,
        adapter_up_gradient,
    )


def solution(mesh):
    in_specs = (
        P(("rep", "seq", "sub"), "head"),
        P(("rep", "seq", "sub"), "head"),
        P(("rep", "seq", "sub"), "head"),
        P(("rep", "seq", "sub"), "head"),
        P("head", "sub"),
        P("head", None),
        P(),
    )
    out_specs = (
        P(("rep", "seq", "sub"), "head"),
        P(("rep", "seq", "sub"), "head"),
        P(("rep", "seq", "sub"), "head"),
        P(("rep", "head"), None),
        P("rep", "head"),
    )
    return jax.shard_map(
        on_device, mesh=mesh, in_specs=in_specs, out_specs=out_specs, check_vma=False
    )
```

profile of v0, /device:TPU:0, one launch (start us, length us, event | category | flops | bytes accessed | tf_op | source)
XLA Modules:
  0.0 434.3 jit_solution(16442148612122126601)
XLA Ops:
  8.7 24.9 %all-gather.3.cloned.1.call-done = bf16[128,4096]{1,0:T(8,128)(2,1)} async-done(((bf16[128,2048]{1,0:T(8,128)(2,1)}), bf16[128,4096]{1,0:T(8,128)(2,1)}) %all-gather.3.cloned.1.call-update) | async-done | bytes 1048592 | tf_op jit(solution)/shard_map/all_gather | solution.py:97
  33.6 1.6 fusion.64
  35.2 19.8 %all-gather.5.cloned.1.call-done = bf16[1024,4096]{1,0:T(8,128)(2,1)} async-done(((bf16[1024,2048]{1,0:T(8,128)(2,1)}), bf16[1024,4096]{1,0:T(8,128)(2,1)}) %all-gather.5.cloned.1.call-update) | async-done | bytes 8388624 | tf_op jit(solution)/shard_map/all_gather | solution.py:100
  55.0 6.6 %fusion.63 = f32[128,1024]{1,0:T(8,128)S(1)} fusion(bf16[128,4096]{1,0:T(8,128)(2,1)} %all-gather.3.cloned.1.call-done, bf16[1024,4096]{1,0:T(8,128)(2,1)} %all-gather.5.cloned.1.call-done), kind=kOutput, calls=%fused_computation.133 | convolution fusion | flops 1073741824 | bytes 9961472 | tf_op jit(solution)/shard_map/dot_general | solution.py:98
  63.0 4.6 %all_to_all.30 = bf16[4,128,1024]{1,0,2:T(4,128)(2,1)S(1)} all-to-all(bf16[4,128,1024]{1,0,2:T(4,128)(2,1)S(1)} %copy.81), channel_id=1, replica_groups=mesh['rep'=1,'seq'=8,'head'=2,'sub'=2] {'sub'}, dimensions={2} | all-to-all | bytes 2097152 | tf_op jit(solution)/shard_map/all_to_all | solution.py:120
  68.0 4.6 %collective-permute-start = (bf16[2,256,512]{2,1,0:T(8,128)(2,1)S(1)}, bf16[2,256,512]{2,1,0:T(8,128)(2,1)S(1)}, u32[]{:S(2)}, u32[]{:S(2)}) collective-permute-start(bf16[2,256,512]{2,1,0:T(8,128)(2,1)S(1)} %bitcast.158), channel_id=1, source_target_pairs={{0,28},{4,0},{8,4},{12,8},{16,12},{20,16},{24,20},{28,24},{1,29},{... | collective-permute-start | bytes 1572872 | tf_op jit(solution)/shard_map/ppermute | solution.py:12
  74.4 2.9 collective-permute-start.3
  77.3 7.6 %collective-permute-done = bf16[2,256,512]{2,1,0:T(8,128)(2,1)S(1)} collective-permute-done((bf16[2,256,512]{2,1,0:T(8,128)(2,1)S(1)}, bf16[2,256,512]{2,1,0:T(8,128)(2,1)S(1)}, u32[]{:S(2)}, u32[]{:S(2)}) %collective-permute-start) | collective-permute-done | bytes 524320 | tf_op jit(solution)/shard_map/ppermute | solution.py:12
  88.1 8.0 %collective-permute-done.1 = bf16[2,256,512]{2,1,0:T(8,128)(2,1)} collective-permute-done((bf16[2,256,512]{2,1,0:T(8,128)(2,1)S(1)}, bf16[2,256,512]{2,1,0:T(8,128)(2,1)}, u32[]{:S(2)}, u32[]{:S(2)}) %collective-permute-start.1) | collective-permute-done | bytes 524320 | tf_op jit(solution)/shard_map/ppermute | solution.py:12
  96.2 1.2 copy.86
  99.2 8.3 %collective-permute-done.2 = bf16[2,256,512]{2,1,0:T(8,128)(2,1)} collective-permute-done((bf16[2,256,512]{2,1,0:T(8,128)(2,1)S(1)}, bf16[2,256,512]{2,1,0:T(8,128)(2,1)}, u32[]{:S(2)}, u32[]{:S(2)}) %collective-permute-start.2) | collective-permute-done | bytes 524320 | tf_op jit(solution)/shard_map/ppermute | solution.py:12
  107.5 1.2 copy.87
  108.7 54.2 %collective-permute-done.3 = bf16[2,256,512]{2,1,0:T(8,128)(2,1)} collective-permute-done((bf16[2,256,512]{2,1,0:T(8,128)(2,1)S(1)}, bf16[2,256,512]{2,1,0:T(8,128)(2,1)}, u32[]{:S(2)}, u32[]{:S(2)}) %collective-permute-start.3) | collective-permute-done | bytes 524320 | tf_op jit(solution)/shard_map/ppermute | solution.py:12
  162.9 1.2 copy.88
  164.1 1.2 copy.89
  165.4 1.2 copy.90
  170.2 1.2 copy.91
  173.2 6.2 %copy.95 = bf16[4,2,2048,128]{3,2,1,0:T(8,128)(2,1)} copy(bf16[4,2,2048,128]{2,3,0,1:T(8,128)(2,1)} %bitcast.16) | data formatting | bytes 8388608
  180.1 42.8 %while.25 = (s32[]{:T(128)}, bf16[4,256,128]{1,2,0:T(8,128)(2,1)}, bf16[4,2,2048,128]{2,3,0,1:T(8,128)(2,1)}, bf16[4,256,128]{2,1,0:T(8,128)(2,1)S(1)}, bf16[4,2...) while((s32[]{:T(128)}, bf16[4,256,128]{1,2,0:T(8,128)(2,1)}, ...), condition=%wide.region_8.9_spmd.clone, body=%wide.region_4.8_spmd.clone.sunk | while | flops 706772224 | bytes 27380468 | solution.py:75
  180.1 1.9 fusion.101
  182.4 1.7 multiply_reduce_fusion.2
  184.9 1.5 fusion.103
  187.1 1.5 fusion.104
  189.8 1.1 constant_dynamic-update-slice_fusion.16
  190.8 1.9 fusion.101
  193.1 1.7 multiply_reduce_fusion.2
  195.6 1.5 fusion.103
  197.8 1.5 fusion.104
  200.5 1.1 constant_dynamic-update-slice_fusion.16
  201.5 1.9 fusion.101
  203.8 1.7 multiply_reduce_fusion.2
  206.3 1.5 fusion.103
  208.5 1.5 fusion.104
  211.1 1.1 constant_dynamic-update-slice_fusion.16
  212.2 1.9 fusion.101
  214.5 1.7 multiply_reduce_fusion.2
  217.0 1.5 fusion.103
  219.2 1.5 fusion.104
  221.9 1.1 constant_dynamic-update-slice_fusion.16
  223.0 3.5 fusion.60
  226.5 2.3 collective-permute-start.11
  228.8 3.0 collective-permute-start.10
  231.7 12.5 %collective-permute-done.13 = bf16[2,256,512]{1,2,0:T(8,128)(2,1)S(1)} collective-permute-done((bf16[2,256,512]{1,2,0:T(8,128)(2,1)S(1)}, bf16[2,256,512]{1,2,0:T(8,128)(2,1)S(1)}, u32[]{:S(2)}, u32[]{:S(2)}) %collective-permute-start.13) | collective-permute-done | bytes 524320 | tf_op jit(solution)/shard_map/ppermute | solution.py:12
  244.2 10.7 %collective-permute-start.7 = (bf16[2,256,512]{1,2,0:T(8,128)(2,1)S(1)}, bf16[2,256,512]{1,2,0:T(8,128)(2,1)}, u32[]{:S(2)}, u32[]{:S(2)}) collective-permute-start(bf16[2,256,512]{1,2,0:T(8,128)(2,1)S(1)} %get-tuple-element.306), channel_id=1, source_target_pairs={{0,28},{4,0},{8,4},{12,8},{16,12},{20,16},{24,20},{28,24},{1,29},{... | collective-permute-start | bytes 1572872 | tf_op jit(solution)/shard_map/ppermute | solution.py:12
  254.9 16.3 %while.24 = (s32[]{:T(128)}, bf16[4,256,128]{1,2,0:T(8,128)(2,1)S(1)}, bf16[4,256,128]{2,1,0:T(8,128)(2,1)S(1)}, bf16[4,2,2048,128]{3,2,1,0:T(8,128)(2,1)}, s32[...) while((s32[]{:T(128)}, ...), condition=%wide.region_3.4_spmd.clone, body=%wide.region_0.3_spmd.clone.sunk | while | flops 297827840 | bytes 7761061 | solution.py:72
  254.9 1.9 fusion.93
  257.2 1.6 fusion.95
  259.0 1.9 fusion.93
  261.3 1.6 fusion.95
  263.1 1.9 fusion.93
  265.4 1.6 fusion.95
  267.2 1.9 fusion.93
  269.5 1.6 fusion.95
  271.3 16.2 %collective-permute-done.11 = bf16[2,256,512]{1,2,0:T(8,128)(2,1)} collective-permute-done((bf16[2,256,512]{1,2,0:T(8,128)(2,1)}, bf16[2,256,512]{1,2,0:T(8,128)(2,1)}, u32[]{:S(2)}, u32[]{:S(2)}) %collective-permute-start.11) | collective-permute-done | bytes 524320 | tf_op jit(solution)/shard_map/ppermute | solution.py:12
  287.5 6.1 %collective-permute-done.7 = bf16[2,256,512]{1,2,0:T(8,128)(2,1)} collective-permute-done((bf16[2,256,512]{1,2,0:T(8,128)(2,1)S(1)}, bf16[2,256,512]{1,2,0:T(8,128)(2,1)}, u32[]{:S(2)}, u32[]{:S(2)}) %collective-permute-start.7) | collective-permute-done | bytes 524320 | tf_op jit(solution)/shard_map/ppermute | solution.py:12
  293.6 2.7 add_convert_fusion
  296.4 1.0 copy.103
  297.5 4.6 %all_to_all.31 = bf16[4,256,512]{2,0,1:T(4,128)(2,1)S(1)} all-to-all(bf16[4,256,512]{2,0,1:T(4,128)(2,1)S(1)} %copy.103), channel_id=1, replica_groups=mesh['rep'=1,'seq'=8,'head'=2,'sub'=2] {'sub'}, dimensions={1} | all-to-all | bytes 2097152 | tf_op jit(solution)/shard_map/all_to_all | solution.py:137
  302.7 0.9 convolution_multiply_fusion.4
  303.8 5.1 %psum.22 = f32[128,16]{0,1:T(8,128)S(1)} all-reduce(f32[128,16]{0,1:T(8,128)S(1)} %fusion.65), channel_id=1, replica_groups=mesh['rep'=1,'seq'=8,'head'=2,'sub'=2] {'head'}, use_global_device_ids=true, to_apply=%region_10.11 | all-reduce | flops 2048 | bytes 16384 | tf_op jit(solution)/shard_map/psum | solution.py:148
  309.0 1.0 convolution_multiply_fusion.2
  313.1 111.7 %all-reduce.3.cloned.1.call-done = (f32[1024,16]{0,1:T(8,128)}, f32[16,2048]{1,0:T(8,128)}) async-done(((f32[1024,16]{0,1:T(8,128)}, f32[16,2048]{1,0:T(8,128)}), (f32[1024,16]{0,1:T(8,128)}, f32[16,2048]{1,0:T(8,128)})) %all-reduce.3.cloned.1.call-update) | async-done | bytes 196624 | tf_op jit(solution)/shard_map/psum | solution.py:152
  424.8 1.5 copy.153
  426.2 1.6 copy.154
  (150 shorter events, 34.2 us)
Async XLA Ops:
  7.2 26.4 %copy-start = (bf16[16,4096]{1,0:T(8,128)(2,1)S(1)}, bf16[16,4096]{1,0:T(8,128)(2,1)}, u32[]{:S(2)}) copy-start(bf16[16,4096]{1,0:T(8,128)(2,1)} %param.17) | copy-start | bytes 393220
  7.2 26.4 %all-gather.3.cloned.1.call-start = ((), (), s32[]{:S(2)}) async-start(), calls=%async_computation.2 | async-start | bytes 1572864 | tf_op jit(solution)/shard_map/all_gather | solution.py:97
  7.9 47.1 %all-gather.5.cloned.1.call-start = ((), (), s32[]{:S(2)}) async-start(), calls=%async_computation.3 | async-start | bytes 12582912 | tf_op jit(solution)/shard_map/all_gather | solution.py:100
  8.7 416.1 %all-reduce.3.cloned.1.call-start = ((), (), s32[]{:S(2)}) async-start(), calls=%async_computation.4 | async-start | bytes 393216 | tf_op jit(solution)/shard_map/psum | solution.py:152
  35.2 26.5 %copy-start.13 = (f32[128,16]{0,1:T(8,128)}, f32[128,16]{0,1:T(8,128)S(1)}, u32[]{:S(2)}) copy-start(f32[128,16]{0,1:T(8,128)S(1)} %fusion.64) | copy-start | bytes 24580
  35.2 26.5 %copy-start.11 = (bf16[1024,16]{0,1:T(8,128)(2,1)S(1)}, bf16[1024,16]{0,1:T(8,128)(2,1)}, u32[]{:S(2)}) copy-start(bf16[1024,16]{0,1:T(8,128)(2,1)} %param.16) | copy-start | bytes 98308
  35.2 26.9 %copy-start.8 = (bf16[128,1024]{1,0:T(8,128)(2,1)S(1)}, bf16[128,1024]{1,0:T(8,128)(2,1)}, u32[]{:S(2)}) copy-start(bf16[128,1024]{1,0:T(8,128)(2,1)} %param.13) | copy-start | bytes 786436
  35.2 26.9 %copy-start.9 = (bf16[128,1024]{1,0:T(8,128)(2,1)S(1)}, bf16[128,1024]{1,0:T(8,128)(2,1)}, u32[]{:S(2)}) copy-start(bf16[128,1024]{1,0:T(8,128)(2,1)} %param.12) | copy-start | bytes 786436
  35.2 26.9 %copy-start.10 = (bf16[128,1024]{1,0:T(8,128)(2,1)S(1)}, bf16[128,1024]{1,0:T(8,128)(2,1)}, u32[]{:S(2)}) copy-start(bf16[128,1024]{1,0:T(8,128)(2,1)} %param.11) | copy-start | bytes 786436
  68.0 16.9 %collective-permute-start = (bf16[2,256,512]{2,1,0:T(8,128)(2,1)S(1)}, bf16[2,256,512]{2,1,0:T(8,128)(2,1)S(1)}, u32[]{:S(2)}, u32[]{:S(2)}) collective-permute-start(bf16[2,256,512]{2,1,0:T(8,128)(2,1)S(1)} %bitcast.158), channel_id=1, source_target_pairs={{0,28},{4,0},{8,4},{12,8},{16,12},{20,16},{24,20},{28,24},{1,29},{... | collective-permute-start | bytes 1572872 | tf_op jit(solution)/shard_map/ppermute | solution.py:12
  72.6 23.6 %collective-permute-start.1 = (bf16[2,256,512]{2,1,0:T(8,128)(2,1)S(1)}, bf16[2,256,512]{2,1,0:T(8,128)(2,1)}, u32[]{:S(2)}, u32[]{:S(2)}) collective-permute-start(bf16[2,256,512]{2,1,0:T(8,128)(2,1)S(1)} %bitcast.159), channel_id=1, source_target_pairs={{0,24},{4,28},{8,0},{12,4},{16,8},{20,12},{24,16},{28,20},{1,25},{... | collective-permute-start | bytes 1572872 | tf_op jit(solution)/shard_map/ppermute | solution.py:12
  74.4 33.1 %collective-permute-start.2 = (bf16[2,256,512]{2,1,0:T(8,128)(2,1)S(1)}, bf16[2,256,512]{2,1,0:T(8,128)(2,1)}, u32[]{:S(2)}, u32[]{:S(2)}) collective-permute-start(bf16[2,256,512]{2,1,0:T(8,128)(2,1)S(1)} %bitcast.160), channel_id=1, source_target_pairs={{0,20},{4,24},{8,28},{12,0},{16,4},{20,8},{24,12},{28,16},{1,21},{... | collective-permute-start | bytes 1572872 | tf_op jit(solution)/shard_map/ppermute | solution.py:12
  74.4 88.5 %collective-permute-start.3 = (bf16[2,256,512]{2,1,0:T(8,128)(2,1)S(1)}, bf16[2,256,512]{2,1,0:T(8,128)(2,1)}, u32[]{:S(2)}, u32[]{:S(2)}) collective-permute-start(bf16[2,256,512]{2,1,0:T(8,128)(2,1)S(1)} %bitcast.161), channel_id=1, source_target_pairs={{0,16},{4,20},{8,24},{12,28},{16,0},{20,4},{24,8},{28,12},{1,17},{... | collective-permute-start | bytes 1572872 | tf_op jit(solution)/shard_map/ppermute | solution.py:12
  77.3 86.8 %collective-permute-start.4 = (bf16[2,256,512]{2,1,0:T(8,128)(2,1)S(1)}, bf16[2,256,512]{2,1,0:T(8,128)(2,1)}, u32[]{:S(2)}, u32[]{:S(2)}) collective-permute-start(bf16[2,256,512]{2,1,0:T(8,128)(2,1)S(1)} %bitcast.162), channel_id=1, source_target_pairs={{0,12},{4,16},{8,20},{12,24},{16,28},{20,0},{24,4},{28,8},{1,13},{... | collective-permute-start | bytes 1572872 | tf_op jit(solution)/shard_map/ppermute | solution.py:12
  85.0 0.8 copy-start.6
  85.0 80.4 %collective-permute-start.5 = (bf16[2,256,512]{2,1,0:T(8,128)(2,1)S(1)}, bf16[2,256,512]{2,1,0:T(8,128)(2,1)}, u32[]{:S(2)}, u32[]{:S(2)}) collective-permute-start(bf16[2,256,512]{2,1,0:T(8,128)(2,1)S(1)} %bitcast.163), channel_id=1, source_target_pairs={{0,8},{4,12},{8,16},{12,20},{16,24},{20,28},{24,0},{28,4},{1,9},{5... | collective-permute-start | bytes 1572872 | tf_op jit(solution)/shard_map/ppermute | solution.py:12
  86.4 1.6 copy-start.7
  96.2 74.0 %collective-permute-start.6 = (bf16[2,256,512]{2,1,0:T(8,128)(2,1)S(1)}, bf16[2,256,512]{2,1,0:T(8,128)(2,1)}, u32[]{:S(2)}, u32[]{:S(2)}) collective-permute-start(bf16[2,256,512]{2,1,0:T(8,128)(2,1)S(1)} %bitcast.164), channel_id=1, source_target_pairs={{0,4},{4,8},{8,12},{12,16},{16,20},{20,24},{24,28},{28,0},{1,5},{5... | collective-permute-start | bytes 1572872 | tf_op jit(solution)/shard_map/ppermute | solution.py:12
  180.1 1.9 copy-start.15
  189.2 1.6 copy-start.16
  190.8 1.9 copy-start.15
  199.9 1.6 copy-start.16
  201.5 1.9 copy-start.15
  210.6 1.6 copy-start.16
  212.2 1.9 copy-start.15
  221.3 1.7 copy-start.16
  226.5 17.8 %collective-permute-start.13 = (bf16[2,256,512]{1,2,0:T(8,128)(2,1)S(1)}, bf16[2,256,512]{1,2,0:T(8,128)(2,1)S(1)}, u32[]{:S(2)}, u32[]{:S(2)}) collective-permute-start(bf16[2,256,512]{1,2,0:T(8,128)(2,1)S(1)} %get-tuple-element.307), channel_id=1, source_target_pairs={{0,4},{4,8},{8,12},{12,16},{16,20},{20,24},{24,28},{28,0},{1,5},{5... | collective-permute-start | bytes 1572872 | tf_op jit(solution)/shard_map/ppermute | solution.py:12
  226.5 17.8 %collective-permute-start.12 = (bf16[2,256,512]{1,2,0:T(8,128)(2,1)S(1)}, bf16[2,256,512]{1,2,0:T(8,128)(2,1)S(1)}, u32[]{:S(2)}, u32[]{:S(2)}) collective-permute-start(bf16[2,256,512]{1,2,0:T(8,128)(2,1)S(1)} %get-tuple-element.308), channel_id=1, source_target_pairs={{0,8},{4,12},{8,16},{12,20},{16,24},{20,28},{24,0},{28,4},{1,9},{5... | collective-permute-start | bytes 1572872 | tf_op jit(solution)/shard_map/ppermute | solution.py:12
  226.5 61.0 %collective-permute-start.11 = (bf16[2,256,512]{1,2,0:T(8,128)(2,1)}, bf16[2,256,512]{1,2,0:T(8,128)(2,1)}, u32[]{:S(2)}, u32[]{:S(2)}) collective-permute-start(bf16[2,256,512]{1,2,0:T(8,128)(2,1)} %get-tuple-element.309), channel_id=1, source_target_pairs={{0,12},{4,16},{8,20},{12,24},{16,28},{20,0},{24,4},{28,8},{1,13},{... | collective-permute-start | bytes 1572872 | tf_op jit(solution)/shard_map/ppermute | solution.py:12
  228.8 58.7 %collective-permute-start.10 = (bf16[2,256,512]{1,2,0:T(8,128)(2,1)}, bf16[2,256,512]{1,2,0:T(8,128)(2,1)}, u32[]{:S(2)}, u32[]{:S(2)}) collective-permute-start(bf16[2,256,512]{1,2,0:T(8,128)(2,1)} %get-tuple-element.310), channel_id=1, source_target_pairs={{0,16},{4,20},{8,24},{12,28},{16,0},{20,4},{24,8},{28,12},{1,17},{... | collective-permute-start | bytes 1572872 | tf_op jit(solution)/shard_map/ppermute | solution.py:12
  231.7 55.7 %collective-permute-start.9 = (bf16[2,256,512]{1,2,0:T(8,128)(2,1)}, bf16[2,256,512]{1,2,0:T(8,128)(2,1)}, u32[]{:S(2)}, u32[]{:S(2)}) collective-permute-start(bf16[2,256,512]{1,2,0:T(8,128)(2,1)} %get-tuple-element.311), channel_id=1, source_target_pairs={{0,20},{4,24},{8,28},{12,0},{16,4},{20,8},{24,12},{28,16},{1,21},{... | collective-permute-start | bytes 1572872 | tf_op jit(solution)/shard_map/ppermute | solution.py:12
  244.2 10.7 %copy-start.4 = (bf16[2,256,512]{1,2,0:T(8,128)(2,1)}, bf16[2,256,512]{1,2,0:T(8,128)(2,1)S(1)}, u32[]{:S(2)}) copy-start(bf16[2,256,512]{1,2,0:T(8,128)(2,1)S(1)} %collective-permute-done.13) | copy-start | bytes 1572868
  244.2 43.3 %collective-permute-start.8 = (bf16[2,256,512]{1,2,0:T(8,128)(2,1)}, bf16[2,256,512]{1,2,0:T(8,128)(2,1)}, u32[]{:S(2)}, u32[]{:S(2)}) collective-permute-start(bf16[2,256,512]{1,2,0:T(8,128)(2,1)} %get-tuple-element.312), channel_id=1, source_target_pairs={{0,24},{4,28},{8,0},{12,4},{16,8},{20,12},{24,16},{28,20},{1,25},{... | collective-permute-start | bytes 1572872 | tf_op jit(solution)/shard_map/ppermute | solution.py:12
  244.2 10.7 %copy-start.5 = (bf16[2,256,512]{1,2,0:T(8,128)(2,1)}, bf16[2,256,512]{1,2,0:T(8,128)(2,1)S(1)}, u32[]{:S(2)}) copy-start(bf16[2,256,512]{1,2,0:T(8,128)(2,1)S(1)} %collective-permute-done.12) | copy-start | bytes 1572868
  244.2 49.4 %collective-permute-start.7 = (bf16[2,256,512]{1,2,0:T(8,128)(2,1)S(1)}, bf16[2,256,512]{1,2,0:T(8,128)(2,1)}, u32[]{:S(2)}, u32[]{:S(2)}) collective-permute-start(bf16[2,256,512]{1,2,0:T(8,128)(2,1)S(1)} %get-tuple-element.306), channel_id=1, source_target_pairs={{0,28},{4,0},{8,4},{12,8},{16,12},{20,16},{24,20},{28,24},{1,29},{... | collective-permute-start | bytes 1572872 | tf_op jit(solution)/shard_map/ppermute | solution.py:12
  271.2 25.1 %copy-start.3 = (bf16[4,256,128]{1,2,0:T(8,128)(2,1)S(1)}, bf16[4,256,128]{1,2,0:T(8,128)(2,1)}, u32[]{:S(2)}) copy-start(bf16[4,256,128]{1,2,0:T(8,128)(2,1)} %get-tuple-element.71) | copy-start | bytes 786436
  302.0 0.7 copy-start.14
  302.0 1.6 copy-start.12
  302.2 6.7 %copy-start.2 = (bf16[128,2048]{1,0:T(8,128)(2,1)S(1)}, bf16[128,2048]{1,0:T(8,128)(2,1)}, u32[]{:S(2)}) copy-start(bf16[128,2048]{1,0:T(8,128)(2,1)} %param.14) | copy-start | bytes 1572868
  303.8 124.0 %copy-start.1 = (bf16[16,4096]{1,0:T(8,128)(2,1)S(1)}, bf16[16,4096]{1,0:T(8,128)(2,1)}, u32[]{:S(2)}) copy-start(bf16[16,4096]{1,0:T(8,128)(2,1)} %param.17) | copy-start | bytes 393220
Sparse Core Ops, SparseCore 0:
  9.6 23.9 all-gather.2
  35.1 19.8 all-gather.4
  310.1 114.6 all-reduce.2
where the time goes:
time: 436 us; the launch traced here: 434 us
  waiting for transfers between devices  271 us (62%)
  matrix products  52.9 us (12%)
  local copies, waits for them, and re-layouts  46.3 us (11%)
  starting transfers between devices  24.1 us (6%)
  blocking collectives  14.3 us (3%)
  between operations  14.1 us (3%)
  other arithmetic  11.4 us (3%)
    ppermute x14, waiting for transfers between devices, passed_along(): lax.ppermute(value, axis, [(i, (i + by) % peers) for i in range(peers)])  113 us
    psum x1, waiting for transfers between devices, on_device(): lax.psum((down_gradient_part, up_gradient_part), ('seq', 'sub'))  112 us
    all_gather x1, waiting for transfers between devices, on_device(): total_gradient = lax.all_gather(output_gradient, 'head', axis=1, tiled=True)  24.9 us
    ppermute x14, starting transfers between devices, passed_along(): lax.ppermute(value, axis, [(i, (i + by) % peers) for i in range(peers)])  24 us
    all_gather x1, waiting for transfers between devices, on_device(): lax.all_gather(output_matrix, 'sub', axis=1, tiled=True)  19.8 us
    unnamed x45, local copies, waits for them, and re-layouts  19.2 us
    dot_general x8, matrix products, softmax_rows(): lax.dot_general(query_head, keys_head, (((1,), (1,)), ((), ())), preferre...  14.9 us
  transfers between devices with their start and end apart: 17, of which 10 were waited for; matrix products, arithmetic and copies ran while one was open for 8% of the time, Pallas kernels for 0%

commit v1 on v0

--- a/solution.py
+++ b/solution.py
@@ -5,6 +5,23 @@
 
 HD = 128
 GROUP = 2048
+
+
+def laid_out(blocks, dim):
+    blocks = jnp.moveaxis(blocks, 0, dim)
+    shape = blocks.shape
+    return blocks.reshape(*shape[:dim], shape[dim] * shape[dim + 1], *shape[dim + 2 :])
+
+
+def doubled(x, axis):
+    size, index = (lax.axis_size(axis), lax.axis_index(axis))
+    parts, stride = (x[None], 1)
+    while stride < size:
+        other = lax.ppermute(parts, axis, [(i, i ^ stride) for i in range(size)])
+        low = index & stride == 0
+        parts = jnp.concatenate([jnp.where(low, parts, other), jnp.where(low, other, parts)])
+        stride *= 2
+    return parts
 
 
 def passed_along(value, axis, by):
@@ -94,7 +111,7 @@
     tokens_dev, feat_dev = head_query_rows.shape
     head_index = lax.axis_index("head")
     shifted = head_index >= lax.axis_size("head") // 2
-    total_gradient = lax.all_gather(output_gradient, "head", axis=1, tiled=True)
+    total_gradient = laid_out(doubled(output_gradient, "head"), 1)
     projected_output = lax.dot_general(
         total_gradient,
         lax.all_gather(output_matrix, "sub", axis=1, tiled=True),

time: 436 us -> 413 us (0.947)
  waiting for transfers between devices: 271 us -> 245 us
    all_gather x1 -> x0, waiting for transfers between devices: 24.9 us -> none  [on_device(): total_gradient = lax.all_gather(output_gradient, 'head', axis=1, tiled=True)]
    all_gather x1, waiting for transfers between devices: 19.8 us -> 7.17 us  [on_device(): lax.all_gather(output_matrix, 'sub', axis=1, tiled=True)]
    ppermute x0 -> x1, waiting for transfers between devices: none -> 11.9 us  [doubled(): other = lax.ppermute(parts, axis, [(i, i ^ stride) for i in range(size)])]
    unnamed x45 -> x44, local copies, waits for them, and re-layouts: 19.2 us -> 20.2 us
  transfers between devices with their start and end apart: 17 -> 17, of which waited for: 10 -> 10; matrix products, arithmetic and copies ran while one was open for 8% -> 9% of each run, Pallas kernels for 0% -> 0%
where the time goes in v1:
time: 413 us; the launch traced here: 411 us
  waiting for transfers between devices  245 us (59%)
  matrix products  51.2 us (12%)
  local copies, waits for them, and re-layouts  47.3 us (11%)
  starting transfers between devices  27.1 us (7%)
  between operations  14.4 us (3%)
  blocking collectives  14.3 us (3%)
  other arithmetic  11.4 us (3%)
    ppermute x14, waiting for transfers between devices, passed_along(): lax.ppermute(value, axis, [(i, (i + by) % peers) for i in range(peers)])  113 us
    psum x1, waiting for transfers between devices, on_device(): lax.psum((down_gradient_part, up_gradient_part), ('seq', 'sub'))  112 us
    ppermute x14, starting transfers between devices, passed_along(): lax.ppermute(value, axis, [(i, (i + by) % peers) for i in range(peers)])  24 us
    unnamed x44, local copies, waits for them, and re-layouts  20.2 us
    dot_general x8, matrix products, softmax_rows(): lax.dot_general(query_head, keys_head, (((1,), (1,)), ((), ())), preferre...  14.9 us
    ppermute x1, waiting for transfers between devices, doubled(): other = lax.ppermute(parts, axis, [(i, i ^ stride) for i in range(size)])  11.9 us
  transfers between devices with their start and end apart: 17, of which 10 were waited for; matrix products, arithmetic and copies ran while one was open for 9% of the time, Pallas kernels for 0%

profile of v1, /device:TPU:0, one launch (start us, length us, event | category | flops | bytes accessed | tf_op | source)
XLA Modules:
  0.0 410.9 jit_solution(16694369452434849404)
XLA Ops:
  8.5 3.0 collective-permute-start
  11.5 11.9 %collective-permute-done = bf16[1,128,2048]{1,2,0:T(8,128)(2,1)S(1)} collective-permute-done((bf16[1,128,2048]{1,2,0:T(8,128)(2,1)S(1)}, bf16[1,128,2048]{1,2,0:T(8,128)(2,1)S(1)}, u32[]{:S(2)}, u32[]{:S(2)}) %collective-permute-start) | collective-permute-done | bytes 524320 | tf_op jit(solution)/shard_map/ppermute | solution.py:20
  25.0 7.2 %all-gather.2.cloned.1.call-done = bf16[1024,4096]{1,0:T(8,128)(2,1)} async-done(((bf16[1024,2048]{1,0:T(8,128)(2,1)}), bf16[1024,4096]{1,0:T(8,128)(2,1)}) %all-gather.2.cloned.1.call-update) | async-done | bytes 8388624 | tf_op jit(solution)/shard_map/all_gather | solution.py:117
  32.2 6.3 %fusion.54 = bf16[1,128,1024]{2,1,0:T(8,128)(2,1)S(1)} fusion(f32[128,1024]{1,0:T(8,128)S(1)} %convolution_multiply_fusion.3, bf16[128,4096]{0,1:T(8,128)(2,1)S(1)} %bitcast.144, bf16[1024,4096]{1,0:T(8,128)(2,1)} %all-gather.2.cloned.1.call-done), kind=kOutput, calls=%fused_computation.105 | convolution fusion | flops 1074003968 | bytes 10223616 | tf_op jit(solution)/shard_map/dot_general | solution.py:115
  39.4 4.6 %all_to_all.30 = bf16[4,128,1024]{1,0,2:T(4,128)(2,1)S(1)} all-to-all(bf16[4,128,1024]{1,0,2:T(4,128)(2,1)S(1)} %copy.85), channel_id=1, replica_groups=mesh['rep'=1,'seq'=8,'head'=2,'sub'=2] {'sub'}, dimensions={2} | all-to-all | bytes 2097152 | tf_op jit(solution)/shard_map/all_to_all | solution.py:137
  44.4 4.6 %collective-permute-start.1 = (bf16[2,256,512]{2,1,0:T(8,128)(2,1)S(1)}, bf16[2,256,512]{2,1,0:T(8,128)(2,1)S(1)}, u32[]{:S(2)}, u32[]{:S(2)}) collective-permute-start(bf16[2,256,512]{2,1,0:T(8,128)(2,1)S(1)} %bitcast.167), channel_id=1, source_target_pairs={{0,28},{4,0},{8,4},{12,8},{16,12},{20,16},{24,20},{28,24},{1,29},{... | collective-permute-start | bytes 1572872 | tf_op jit(solution)/shard_map/ppermute | solution.py:29
  50.7 2.9 collective-permute-start.4
  53.6 7.7 %collective-permute-done.1 = bf16[2,256,512]{2,1,0:T(8,128)(2,1)S(1)} collective-permute-done((bf16[2,256,512]{2,1,0:T(8,128)(2,1)S(1)}, bf16[2,256,512]{2,1,0:T(8,128)(2,1)S(1)}, u32[]{:S(2)}, u32[]{:S(2)}) %collective-permute-start.1) | collective-permute-done | bytes 524320 | tf_op jit(solution)/shard_map/ppermute | solution.py:29
  64.3 8.3 %collective-permute-done.2 = bf16[2,256,512]{2,1,0:T(8,128)(2,1)} collective-permute-done((bf16[2,256,512]{2,1,0:T(8,128)(2,1)S(1)}, bf16[2,256,512]{2,1,0:T(8,128)(2,1)}, u32[]{:S(2)}, u32[]{:S(2)}) %collective-permute-start.2) | collective-permute-done | bytes 524320 | tf_op jit(solution)/shard_map/ppermute | solution.py:29
  72.5 1.2 copy.90
  75.5 8.3 %collective-permute-done.3 = bf16[2,256,512]{2,1,0:T(8,128)(2,1)} collective-permute-done((bf16[2,256,512]{2,1,0:T(8,128)(2,1)S(1)}, bf16[2,256,512]{2,1,0:T(8,128)(2,1)}, u32[]{:S(2)}, u32[]{:S(2)}) %collective-permute-start.3) | collective-permute-done | bytes 524320 | tf_op jit(solution)/shard_map/ppermute | solution.py:29
  83.8 1.2 copy.91
  85.1 54.2 %collective-permute-done.4 = bf16[2,256,512]{2,1,0:T(8,128)(2,1)} collective-permute-done((bf16[2,256,512]{2,1,0:T(8,128)(2,1)S(1)}, bf16[2,256,512]{2,1,0:T(8,128)(2,1)}, u32[]{:S(2)}, u32[]{:S(2)}) %collective-permute-start.4) | collective-permute-done | bytes 524320 | tf_op jit(solution)/shard_map/ppermute | solution.py:29
  139.2 1.2 copy.92
  140.5 1.2 copy.93
  141.7 1.2 copy.94
  146.6 1.2 copy.95
  149.6 6.2 %copy.99 = bf16[4,2,2048,128]{3,2,1,0:T(8,128)(2,1)} copy(bf16[4,2,2048,128]{2,3,0,1:T(8,128)(2,1)} %bitcast.20) | data formatting | bytes 8388608
  156.5 42.8 %while.25 = (s32[]{:T(128)}, bf16[4,256,128]{1,2,0:T(8,128)(2,1)}, bf16[4,2,2048,128]{2,3,0,1:T(8,128)(2,1)}, bf16[4,256,128]{2,1,0:T(8,128)(2,1)S(1)}, bf16[4,2...) while((s32[]{:T(128)}, bf16[4,256,128]{1,2,0:T(8,128)(2,1)}, ...), condition=%wide.region_8.9_spmd.clone, body=%wide.region_4.8_spmd.clone.sunk | while | flops 706772224 | bytes 27380468 | solution.py:92
  156.5 1.9 fusion.99
  158.8 1.7 multiply_reduce_fusion.2
  161.2 1.5 fusion.101
  163.4 1.5 fusion.102
  166.1 1.1 constant_dynamic-update-slice_fusion.16
  167.2 1.9 fusion.99
  169.5 1.7 multiply_reduce_fusion.2
  171.9 1.5 fusion.101
  174.1 1.5 fusion.102
  176.8 1.0 constant_dynamic-update-slice_fusion.16
  177.8 1.9 fusion.99
  180.1 1.7 multiply_reduce_fusion.2
  182.6 1.5 fusion.101
  184.8 1.5 fusion.102
  187.4 1.1 constant_dynamic-update-slice_fusion.16
  188.5 1.9 fusion.99
  190.8 1.7 multiply_reduce_fusion.2
  193.2 1.5 fusion.101
  195.5 1.5 fusion.102
  198.1 1.1 constant_dynamic-update-slice_fusion.16
  199.3 3.5 fusion.59
  202.7 2.3 collective-permute-start.12
  205.0 3.0 collective-permute-start.11
  208.0 12.5 %collective-permute-done.14 = bf16[2,256,512]{1,2,0:T(8,128)(2,1)S(1)} collective-permute-done((bf16[2,256,512]{1,2,0:T(8,128)(2,1)S(1)}, bf16[2,256,512]{1,2,0:T(8,128)(2,1)S(1)}, u32[]{:S(2)}, u32[]{:S(2)}) %collective-permute-start.14) | collective-permute-done | bytes 524320 | tf_op jit(solution)/shard_map/ppermute | solution.py:29
  220.5 10.7 %collective-permute-start.8 = (bf16[2,256,512]{1,2,0:T(8,128)(2,1)S(1)}, bf16[2,256,512]{1,2,0:T(8,128)(2,1)}, u32[]{:S(2)}, u32[]{:S(2)}) collective-permute-start(bf16[2,256,512]{1,2,0:T(8,128)(2,1)S(1)} %get-tuple-element.306), channel_id=1, source_target_pairs={{0,28},{4,0},{8,4},{12,8},{16,12},{20,16},{24,20},{28,24},{1,29},{... | collective-permute-start | bytes 1572872 | tf_op jit(solution)/shard_map/ppermute | solution.py:29
  231.2 16.3 %while.24 = (s32[]{:T(128)}, bf16[4,256,128]{1,2,0:T(8,128)(2,1)S(1)}, bf16[4,256,128]{2,1,0:T(8,128)(2,1)S(1)}, bf16[4,2,2048,128]{3,2,1,0:T(8,128)(2,1)}, s32[...) while((s32[]{:T(128)}, ...), condition=%wide.region_3.4_spmd.clone, body=%wide.region_0.3_spmd.clone.sunk | while | flops 297827840 | bytes 7761061 | solution.py:89
  231.2 1.9 fusion.91
  233.5 1.6 fusion.93
  235.3 1.9 fusion.91
  237.6 1.6 fusion.93
  239.4 1.9 fusion.91
  241.7 1.6 fusion.93
  243.4 1.9 fusion.91
  245.8 1.6 fusion.93
  247.5 16.2 %collective-permute-done.12 = bf16[2,256,512]{1,2,0:T(8,128)(2,1)} collective-permute-done((bf16[2,256,512]{1,2,0:T(8,128)(2,1)}, bf16[2,256,512]{1,2,0:T(8,128)(2,1)}, u32[]{:S(2)}, u32[]{:S(2)}) %collective-permute-start.12) | collective-permute-done | bytes 524320 | tf_op jit(solution)/shard_map/ppermute | solution.py:29
  263.7 6.1 %collective-permute-done.8 = bf16[2,256,512]{1,2,0:T(8,128)(2,1)} collective-permute-done((bf16[2,256,512]{1,2,0:T(8,128)(2,1)S(1)}, bf16[2,256,512]{1,2,0:T(8,128)(2,1)}, u32[]{:S(2)}, u32[]{:S(2)}) %collective-permute-start.8) | collective-permute-done | bytes 524320 | tf_op jit(solution)/shard_map/ppermute | solution.py:29
  269.9 2.7 add_convert_fusion
  272.7 1.0 copy.107
  273.7 4.6 %all_to_all.31 = bf16[4,256,512]{2,0,1:T(4,128)(2,1)S(1)} all-to-all(bf16[4,256,512]{2,0,1:T(4,128)(2,1)S(1)} %copy.107), channel_id=1, replica_groups=mesh['rep'=1,'seq'=8,'head'=2,'sub'=2] {'sub'}, dimensions={1} | all-to-all | bytes 2097152 | tf_op jit(solution)/shard_map/all_to_all | solution.py:154
  279.0 0.9 convolution_multiply_fusion.4
  280.1 5.1 %psum.22 = f32[128,16]{0,1:T(8,128)S(1)} all-reduce(f32[128,16]{0,1:T(8,128)S(1)} %fusion.63), channel_id=1, replica_groups=mesh['rep'=1,'seq'=8,'head'=2,'sub'=2] {'head'}, use_global_device_ids=true, to_apply=%region_10.11 | all-reduce | flops 2048 | bytes 16384 | tf_op jit(solution)/shard_map/psum | solution.py:165
  285.2 1.0 convolution_multiply_fusion.2
  289.3 111.7 %all-reduce.3.cloned.1.call-done = (f32[1024,16]{0,1:T(8,128)}, f32[16,2048]{1,0:T(8,128)}) async-done(((f32[1024,16]{0,1:T(8,128)}, f32[16,2048]{1,0:T(8,128)}), (f32[1024,16]{0,1:T(8,128)}, f32[16,2048]{1,0:T(8,128)})) %all-reduce.3.cloned.1.call-update) | async-done | bytes 196624 | tf_op jit(solution)/shard_map/psum | solution.py:169
  401.0 1.5 copy.157
  402.5 1.6 copy.158
  (150 shorter events, 34.8 us)
Async XLA Ops:
  7.2 16.5 %copy-start = (bf16[16,4096]{1,0:T(8,128)(2,1)S(1)}, bf16[16,4096]{1,0:T(8,128)(2,1)}, u32[]{:S(2)}) copy-start(bf16[16,4096]{1,0:T(8,128)(2,1)} %param.17) | copy-start | bytes 393220
  7.2 1.1 copy-start.2
  7.2 25.0 %all-gather.2.cloned.1.call-start = ((), (), s32[]{:S(2)}) async-start(), calls=%async_computation.2 | async-start | bytes 12582912 | tf_op jit(solution)/shard_map/all_gather | solution.py:117
  7.9 393.1 %all-reduce.3.cloned.1.call-start = ((), (), s32[]{:S(2)}) async-start(), calls=%async_computation.3 | async-start | bytes 393216 | tf_op jit(solution)/shard_map/psum | solution.py:169
  8.5 14.9 %collective-permute-start = (bf16[1,128,2048]{1,2,0:T(8,128)(2,1)S(1)}, bf16[1,128,2048]{1,2,0:T(8,128)(2,1)S(1)}, u32[]{:S(2)}, u32[]{:S(2)}) collective-permute-start(bf16[1,128,2048]{1,2,0:T(8,128)(2,1)S(1)} %bitcast.152), channel_id=1, source_target_pairs={{0,2},{2,0},{1,3},{3,1},{4,6},{6,4},{5,7},{7,5},{8,10},{10,8},{9,1... | collective-permute-start | bytes 1572872 | tf_op jit(solution)/shard_map/ppermute | solution.py:20
  23.5 1.0 copy-start.10
  23.9 0.6 copy-start.12
  25.0 13.5 %copy-start.7 = (bf16[128,1024]{1,0:T(8,128)(2,1)S(1)}, bf16[128,1024]{1,0:T(8,128)(2,1)}, u32[]{:S(2)}) copy-start(bf16[128,1024]{1,0:T(8,128)(2,1)} %param.13) | copy-start | bytes 786436
  25.0 13.5 %copy-start.8 = (bf16[128,1024]{1,0:T(8,128)(2,1)S(1)}, bf16[128,1024]{1,0:T(8,128)(2,1)}, u32[]{:S(2)}) copy-start(bf16[128,1024]{1,0:T(8,128)(2,1)} %param.12) | copy-start | bytes 786436
  25.0 13.5 %copy-start.9 = (bf16[128,1024]{1,0:T(8,128)(2,1)S(1)}, bf16[128,1024]{1,0:T(8,128)(2,1)}, u32[]{:S(2)}) copy-start(bf16[128,1024]{1,0:T(8,128)(2,1)} %param.11) | copy-start | bytes 786436
  44.4 16.9 %collective-permute-start.1 = (bf16[2,256,512]{2,1,0:T(8,128)(2,1)S(1)}, bf16[2,256,512]{2,1,0:T(8,128)(2,1)S(1)}, u32[]{:S(2)}, u32[]{:S(2)}) collective-permute-start(bf16[2,256,512]{2,1,0:T(8,128)(2,1)S(1)} %bitcast.167), channel_id=1, source_target_pairs={{0,28},{4,0},{8,4},{12,8},{16,12},{20,16},{24,20},{28,24},{1,29},{... | collective-permute-start | bytes 1572872 | tf_op jit(solution)/shard_map/ppermute | solution.py:29
  48.9 23.6 %collective-permute-start.2 = (bf16[2,256,512]{2,1,0:T(8,128)(2,1)S(1)}, bf16[2,256,512]{2,1,0:T(8,128)(2,1)}, u32[]{:S(2)}, u32[]{:S(2)}) collective-permute-start(bf16[2,256,512]{2,1,0:T(8,128)(2,1)S(1)} %bitcast.168), channel_id=1, source_target_pairs={{0,24},{4,28},{8,0},{12,4},{16,8},{20,12},{24,16},{28,20},{1,25},{... | collective-permute-start | bytes 1572872 | tf_op jit(solution)/shard_map/ppermute | solution.py:29
  50.7 33.1 %collective-permute-start.3 = (bf16[2,256,512]{2,1,0:T(8,128)(2,1)S(1)}, bf16[2,256,512]{2,1,0:T(8,128)(2,1)}, u32[]{:S(2)}, u32[]{:S(2)}) collective-permute-start(bf16[2,256,512]{2,1,0:T(8,128)(2,1)S(1)} %bitcast.169), channel_id=1, source_target_pairs={{0,20},{4,24},{8,28},{12,0},{16,4},{20,8},{24,12},{28,16},{1,21},{... | collective-permute-start | bytes 1572872 | tf_op jit(solution)/shard_map/ppermute | solution.py:29
  50.7 88.5 %collective-permute-start.4 = (bf16[2,256,512]{2,1,0:T(8,128)(2,1)S(1)}, bf16[2,256,512]{2,1,0:T(8,128)(2,1)}, u32[]{:S(2)}, u32[]{:S(2)}) collective-permute-start(bf16[2,256,512]{2,1,0:T(8,128)(2,1)S(1)} %bitcast.170), channel_id=1, source_target_pairs={{0,16},{4,20},{8,24},{12,28},{16,0},{20,4},{24,8},{28,12},{1,17},{... | collective-permute-start | bytes 1572872 | tf_op jit(solution)/shard_map/ppermute | solution.py:29
  53.6 86.9 %collective-permute-start.5 = (bf16[2,256,512]{2,1,0:T(8,128)(2,1)S(1)}, bf16[2,256,512]{2,1,0:T(8,128)(2,1)}, u32[]{:S(2)}, u32[]{:S(2)}) collective-permute-start(bf16[2,256,512]{2,1,0:T(8,128)(2,1)S(1)} %bitcast.171), channel_id=1, source_target_pairs={{0,12},{4,16},{8,20},{12,24},{16,28},{20,0},{24,4},{28,8},{1,13},{... | collective-permute-start | bytes 1572872 | tf_op jit(solution)/shard_map/ppermute | solution.py:29
  61.3 80.5 %collective-permute-start.6 = (bf16[2,256,512]{2,1,0:T(8,128)(2,1)S(1)}, bf16[2,256,512]{2,1,0:T(8,128)(2,1)}, u32[]{:S(2)}, u32[]{:S(2)}) collective-permute-start(bf16[2,256,512]{2,1,0:T(8,128)(2,1)S(1)} %bitcast.172), channel_id=1, source_target_pairs={{0,8},{4,12},{8,16},{12,20},{16,24},{20,28},{24,0},{28,4},{1,9},{5... | collective-permute-start | bytes 1572872 | tf_op jit(solution)/shard_map/ppermute | solution.py:29
  72.5 74.0 %collective-permute-start.7 = (bf16[2,256,512]{2,1,0:T(8,128)(2,1)S(1)}, bf16[2,256,512]{2,1,0:T(8,128)(2,1)}, u32[]{:S(2)}, u32[]{:S(2)}) collective-permute-start(bf16[2,256,512]{2,1,0:T(8,128)(2,1)S(1)} %bitcast.173), channel_id=1, source_target_pairs={{0,4},{4,8},{8,12},{12,16},{16,20},{20,24},{24,28},{28,0},{1,5},{5... | collective-permute-start | bytes 1572872 | tf_op jit(solution)/shard_map/ppermute | solution.py:29
  156.5 1.9 copy-start.14
  165.6 1.6 copy-start.15
  167.2 1.9 copy-start.14
  176.2 1.6 copy-start.15
  177.8 1.9 copy-start.14
  186.9 1.6 copy-start.15
  188.5 1.9 copy-start.14
  197.6 1.7 copy-start.15
  202.7 17.8 %collective-permute-start.14 = (bf16[2,256,512]{1,2,0:T(8,128)(2,1)S(1)}, bf16[2,256,512]{1,2,0:T(8,128)(2,1)S(1)}, u32[]{:S(2)}, u32[]{:S(2)}) collective-permute-start(bf16[2,256,512]{1,2,0:T(8,128)(2,1)S(1)} %get-tuple-element.307), channel_id=1, source_target_pairs={{0,4},{4,8},{8,12},{12,16},{16,20},{20,24},{24,28},{28,0},{1,5},{5... | collective-permute-start | bytes 1572872 | tf_op jit(solution)/shard_map/ppermute | solution.py:29
  202.7 17.8 %collective-permute-start.13 = (bf16[2,256,512]{1,2,0:T(8,128)(2,1)S(1)}, bf16[2,256,512]{1,2,0:T(8,128)(2,1)S(1)}, u32[]{:S(2)}, u32[]{:S(2)}) collective-permute-start(bf16[2,256,512]{1,2,0:T(8,128)(2,1)S(1)} %get-tuple-element.308), channel_id=1, source_target_pairs={{0,8},{4,12},{8,16},{12,20},{16,24},{20,28},{24,0},{28,4},{1,9},{5... | collective-permute-start | bytes 1572872 | tf_op jit(solution)/shard_map/ppermute | solution.py:29
  202.7 61.0 %collective-permute-start.12 = (bf16[2,256,512]{1,2,0:T(8,128)(2,1)}, bf16[2,256,512]{1,2,0:T(8,128)(2,1)}, u32[]{:S(2)}, u32[]{:S(2)}) collective-permute-start(bf16[2,256,512]{1,2,0:T(8,128)(2,1)} %get-tuple-element.309), channel_id=1, source_target_pairs={{0,12},{4,16},{8,20},{12,24},{16,28},{20,0},{24,4},{28,8},{1,13},{... | collective-permute-start | bytes 1572872 | tf_op jit(solution)/shard_map/ppermute | solution.py:29
  205.0 58.7 %collective-permute-start.11 = (bf16[2,256,512]{1,2,0:T(8,128)(2,1)}, bf16[2,256,512]{1,2,0:T(8,128)(2,1)}, u32[]{:S(2)}, u32[]{:S(2)}) collective-permute-start(bf16[2,256,512]{1,2,0:T(8,128)(2,1)} %get-tuple-element.310), channel_id=1, source_target_pairs={{0,16},{4,20},{8,24},{12,28},{16,0},{20,4},{24,8},{28,12},{1,17},{... | collective-permute-start | bytes 1572872 | tf_op jit(solution)/shard_map/ppermute | solution.py:29
  208.0 55.7 %collective-permute-start.10 = (bf16[2,256,512]{1,2,0:T(8,128)(2,1)}, bf16[2,256,512]{1,2,0:T(8,128)(2,1)}, u32[]{:S(2)}, u32[]{:S(2)}) collective-permute-start(bf16[2,256,512]{1,2,0:T(8,128)(2,1)} %get-tuple-element.311), channel_id=1, source_target_pairs={{0,20},{4,24},{8,28},{12,0},{16,4},{20,8},{24,12},{28,16},{1,21},{... | collective-permute-start | bytes 1572872 | tf_op jit(solution)/shard_map/ppermute | solution.py:29
  220.5 10.7 %copy-start.5 = (bf16[2,256,512]{1,2,0:T(8,128)(2,1)}, bf16[2,256,512]{1,2,0:T(8,128)(2,1)S(1)}, u32[]{:S(2)}) copy-start(bf16[2,256,512]{1,2,0:T(8,128)(2,1)S(1)} %collective-permute-done.14) | copy-start | bytes 1572868
  220.5 43.3 %collective-permute-start.9 = (bf16[2,256,512]{1,2,0:T(8,128)(2,1)}, bf16[2,256,512]{1,2,0:T(8,128)(2,1)}, u32[]{:S(2)}, u32[]{:S(2)}) collective-permute-start(bf16[2,256,512]{1,2,0:T(8,128)(2,1)} %get-tuple-element.312), channel_id=1, source_target_pairs={{0,24},{4,28},{8,0},{12,4},{16,8},{20,12},{24,16},{28,20},{1,25},{... | collective-permute-start | bytes 1572872 | tf_op jit(solution)/shard_map/ppermute | solution.py:29
  220.5 10.7 %copy-start.6 = (bf16[2,256,512]{1,2,0:T(8,128)(2,1)}, bf16[2,256,512]{1,2,0:T(8,128)(2,1)S(1)}, u32[]{:S(2)}) copy-start(bf16[2,256,512]{1,2,0:T(8,128)(2,1)S(1)} %collective-permute-done.13) | copy-start | bytes 1572868
  220.5 49.4 %collective-permute-start.8 = (bf16[2,256,512]{1,2,0:T(8,128)(2,1)S(1)}, bf16[2,256,512]{1,2,0:T(8,128)(2,1)}, u32[]{:S(2)}, u32[]{:S(2)}) collective-permute-start(bf16[2,256,512]{1,2,0:T(8,128)(2,1)S(1)} %get-tuple-element.306), channel_id=1, source_target_pairs={{0,28},{4,0},{8,4},{12,8},{16,12},{20,16},{24,20},{28,24},{1,29},{... | collective-permute-start | bytes 1572872 | tf_op jit(solution)/shard_map/ppermute | solution.py:29
  247.5 25.0 %copy-start.4 = (bf16[4,256,128]{1,2,0:T(8,128)(2,1)S(1)}, bf16[4,256,128]{1,2,0:T(8,128)(2,1)}, u32[]{:S(2)}) copy-start(bf16[4,256,128]{1,2,0:T(8,128)(2,1)} %get-tuple-element.71) | copy-start | bytes 786436
  278.3 0.7 copy-start.13
  278.3 1.6 copy-start.11
  278.5 6.7 %copy-start.3 = (bf16[128,2048]{1,0:T(8,128)(2,1)S(1)}, bf16[128,2048]{1,0:T(8,128)(2,1)}, u32[]{:S(2)}) copy-start(bf16[128,2048]{1,0:T(8,128)(2,1)} %param.14) | copy-start | bytes 1572868
  280.1 124.0 %copy-start.1 = (bf16[16,4096]{1,0:T(8,128)(2,1)S(1)}, bf16[16,4096]{1,0:T(8,128)(2,1)}, u32[]{:S(2)}) copy-start(bf16[16,4096]{1,0:T(8,128)(2,1)} %param.17) | copy-start | bytes 393220
Sparse Core Ops, SparseCore 0:
  9.6 22.5 all-gather.1
  286.3 114.6 all-reduce.2
